TPU v7x, 256 devices: a whole 4x4x8 slice. The times are simulated.
256 devices in a mesh: rows: 8 (over y, x_lo), cols: 32 (over z, x_hi, core).
Axes of the slice: x: 4 (x_hi: 2, x_lo: 2; x = x_hi * 2 + x_lo), y: 4, z: 8, core: 2. Of those that a mesh axis runs over, the one named last changes fastest.
Arguments:
- counts: bfloat16 [4096, 262144], P('rows', 'cols'), may hold values from 0 to 12, as said below
- start_a: float32 [4096, 128], P(('rows', 'cols')), may hold values from -0.4 to 0.4
- start_b: float32 [16384, 128], P(('cols', 'rows')), may hold values from -0.4 to 0.4
- start_c: float32 [16, 128], replicated, may hold values from -0.4 to 0.4
Outputs:
- factor_a: float32 [4096, 128], P(('rows', 'cols'))
- factor_b: float32 [16384, 128], P(('cols', 'rows'))
- factor_c: float32 [16, 128], replicated
Inputs may be any that keep to these rules, and one draw needn't show every extreme that they name: counts holds whole numbers.
All inputs are finite; a program needn't handle non-finite values.
Results may differ from a plain program's by a relative error of at most 0.009.
Values may be sent and summed in bfloat16 or wider, within the bound.
No kernel may reach another device: no remote copies, remote signals or barrier semaphores. Data moves between devices by JAX's collectives and lax.ppermute only.
A program may use at most 128 MiB of HBM per device.

v0:
```python
import math
import jax
import jax.numpy as jnp
from jax import lax
from jax.sharding import PartitionSpec as P

ITERS = 2


def local(counts, start_a, start_b, start_c):
    rows_here, flat_width = counts.shape
    depth = start_c.shape[0]
    cols_here = flat_width // depth
    total_i = rows_here * lax.axis_size("rows")
    total_j = cols_here * lax.axis_size("cols")
    rate_a = 0.3 / math.sqrt(total_j * depth)
    rate_b = 0.3 / math.sqrt(total_i * depth)
    rate_c = 0.3 / math.sqrt(total_i * total_j)
    local_a, local_b, shared_c = (start_a, start_b, start_c)
    for iteration in range(ITERS):
        low_a = lax.all_gather(local_a.astype(jnp.bfloat16), "cols", axis=0, tiled=True)
        low_b = lax.all_gather(local_b.astype(jnp.bfloat16), "rows", axis=0, tiled=True)
        low_b_wide = low_b.astype(jnp.float32)
        scaled = (low_b_wide[:, None, :] * shared_c[None, :, :]).astype(jnp.bfloat16)
        scaled = scaled.reshape(cols_here * depth, shared_c.shape[1])
        log_rate = lax.dot_general(
            low_a, scaled, (((1,), (1,)), ((), ())), preferred_element_type=jnp.float32
        )
        residual = (jnp.exp(log_rate) - counts.astype(jnp.float32)).astype(jnp.bfloat16)
        grad_a = jnp.dot(residual, scaled, preferred_element_type=jnp.float32)
        mixed = lax.dot_general(
            residual, low_a, (((0,), (0,)), ((), ())), preferred_element_type=jnp.float32
        )
        mixed = mixed.reshape(cols_here, depth, shared_c.shape[1])
        grad_b = jnp.sum(mixed * shared_c[None, :, :], axis=1)
        grad_c = jnp.sum(mixed * low_b_wide[:, None, :], axis=0)
        summed_a = lax.psum_scatter(grad_a, "cols", scatter_dimension=0, tiled=True)
        summed_b = lax.psum_scatter(grad_b, "rows", scatter_dimension=0, tiled=True)
        local_a = local_a - rate_a * summed_a
        local_b = local_b - rate_b * summed_b
        summed_c = lax.psum(grad_c, ("rows", "cols"))
        shared_c = shared_c - rate_c * summed_c
    return (local_a, local_b, shared_c)


def solution(mesh):
    placed = (P("rows", "cols"), P(("rows", "cols"), None), P(("cols", "rows"), None), P())
    return jax.shard_map(
        local,
        mesh=mesh,
        in_specs=placed,
        out_specs=(P(("rows", "cols"), None), P(("cols", "rows"), None), P()),
        check_vma=False,
    )
```

profile of v0, /device:TPU:32, one launch (start us, length us, event | category | flops | bytes accessed | tf_op | source)
XLA Modules:
  0.0 455.2 jit_solution(1326504930640590621)
XLA Ops:
  7.2 0.0 copy-start.2
  7.2 0.0 copy-start.4
  7.2 0.0 copy-start.5
  7.2 0.0 reduce-scatter.5.cloned.1.call-start
  7.2 12.0 %copy.7 = bf16[512,8192]{0,1:T(8,128)(2,1)} copy(bf16[512,8192]{1,0:T(8,128)(2,1)} %param.4) | data formatting | bytes 16777216 | tf_op args[0]
  19.2 0.0 copy-done.2
  19.2 28.6 %all_gather.12 = bf16[512,128]{1,0:T(8,128)(2,1)S(1)} all-gather(bf16[64,128]{1,0:T(8,128)(2,1)S(1)} %convert_element_type.42), channel_id=1, replica_groups=mesh['rows'=8,'cols'=32] {'rows'}, dimensions={0}, use_global_device_ids=true | all-gather | bytes 147456 | tf_op jit(solution)/shard_map/all_gather | solution.py:22
  47.9 0.0 copy-done.4
  47.9 42.5 %all_gather.13 = bf16[512,128]{1,0:T(8,128)(2,1)S(1)} all-gather(bf16[16,128]{1,0:T(8,128)(2,1)S(1)} %convert_element_type.46), channel_id=1, replica_groups=mesh['rows'=8,'cols'=32] {'cols'}, dimensions={0}, use_global_device_ids=true | all-gather | bytes 135168 | tf_op jit(solution)/shard_map/all_gather | solution.py:21
  90.4 0.0 copy-done.5
  90.4 0.4 multiply_convert_fusion.1
  90.8 5.0 %fusion = bf16[512,8192]{0,1:T(8,128)(2,1)S(1)} fusion(bf16[512,8192]{0,1:T(8,128)(2,1)} %copy.7, bf16[8192,128]{1,0:T(8,128)(2,1)S(1)} %bitcast.22, bf16[512,128]{1,0:T(8,128)(2,1)S(1)} %all_gather.13), kind=kOutput, calls=%fused_computation.2 | convolution fusion | flops 1086324736 | bytes 19005440 | tf_op jit(solution)/shard_map/dot_general | solution.py:26
  95.8 0.0 copy-start
  95.8 3.2 copy-done
  99.0 3.0 fusion.4
  102.1 0.0 reduce-scatter.5.cloned.1.call-update
  102.1 0.0 reduce-scatter.7.cloned.1.call-start
  102.1 8.4 %multiply_reduce_fusion.3 = (f32[512,128]{1,0:T(8,128)}, f32[8192,128]{1,0:T(8,128)}) fusion(f32[16,128]{1,0:T(8,128)S(1)} %copy-done.5, bf16[512,8192]{0,1:T(8,128)(2,1)} %copy-done, bf16[512,128]{1,0:T(8,128)(2,1)S(1)} %all_gather.13), kind=kOutput, calls=%fused_computation.8 | convolution fusion | flops 1075773440 | bytes 12984320 | tf_op jit(solution)/shard_map/dot_general | solution.py:31
  110.5 0.0 reduce-scatter.7.cloned.1.call-update
  110.5 0.0 reduce-scatter.9.cloned.1.call-start
  110.6 2.8 multiply_reduce_fusion.2
  113.4 77.1 %psum.14 = f32[16,128]{1,0:T(8,128)S(1)} all-reduce(f32[16,128]{1,0:T(8,128)S(1)} %multiply_reduce_fusion.2), channel_id=1, replica_groups=mesh['rows'=8,'cols'=32] {'rows','cols'}, use_global_device_ids=true, to_apply=%region_4.0 | all-reduce | flops 2048 | bytes 16384 | tf_op jit(solution)/shard_map/psum | solution.py:41
  190.5 21.8 %reduce-scatter.5.cloned.1.call-done = f32[16,128]{1,0:T(8,128)} async-done(((f32[512,128]{1,0:T(8,128)}), f32[16,128]{1,0:T(8,128)}) %reduce-scatter.5.cloned.1.call-update) | async-done | bytes 8208 | tf_op jit(solution)/shard_map/reduce_scatter | solution.py:37
  212.3 0.7 fusion.3
  213.0 38.0 %all_gather.14 = bf16[512,128]{1,0:T(8,128)(2,1)S(1)} all-gather(bf16[16,128]{1,0:T(8,128)(2,1)S(1)} %fusion.3), channel_id=1, replica_groups=mesh['rows'=8,'cols'=32] {'cols'}, dimensions={0}, use_global_device_ids=true | all-gather | bytes 135168 | tf_op jit(solution)/shard_map/all_gather | solution.py:21
  251.0 2.8 reduce-scatter.7.cloned.1.call-done
  253.8 0.8 fusion.2
  254.6 28.5 %all_gather.15 = bf16[512,128]{1,0:T(8,128)(2,1)S(1)} all-gather(bf16[64,128]{1,0:T(8,128)(2,1)S(1)} %fusion.2), channel_id=1, replica_groups=mesh['rows'=8,'cols'=32] {'rows'}, dimensions={0}, use_global_device_ids=true | all-gather | bytes 147456 | tf_op jit(solution)/shard_map/all_gather | solution.py:22
  283.1 0.4 multiply_convert_fusion
  283.5 5.0 %fusion.1 = bf16[512,8192]{0,1:T(8,128)(2,1)S(1)} fusion(bf16[512,8192]{0,1:T(8,128)(2,1)} %copy.7, bf16[512,128]{1,0:T(8,128)(2,1)S(1)} %all_gather.14, bf16[8192,128]{1,0:T(8,128)(2,1)S(1)} %bitcast.24), kind=kOutput, calls=%fused_computation.3 | convolution fusion | flops 1086324736 | bytes 19005440 | tf_op jit(solution)/shard_map/dot_general | solution.py:26
  288.5 0.0 copy-start.1
  288.5 3.2 copy-done.1
  291.7 3.1 fusion.5
  294.8 0.0 reduce-scatter.9.cloned.1.call-update
  294.8 0.0 reduce-scatter.11.cloned.1.call-start
  294.9 8.4 %multiply_reduce_fusion.1 = (f32[512,128]{1,0:T(8,128)}, f32[8192,128]{1,0:T(8,128)}) fusion(f32[16,128]{1,0:T(8,128)S(1)} %multiply_subtract_fusion.4, bf16[512,8192]{0,1:T(8,128)(2,1)} %copy-done.1, bf16[512,128]{1,0:T(8,128)(2,1)S(1)} %all_gather.14), kind=kOutput, calls=%fused_computation.5 | convolution fusion | flops 1075773440 | bytes 12984320 | tf_op jit(solution)/shard_map/dot_general | solution.py:31
  303.3 0.0 copy-start.6
  303.3 0.0 copy-start.3
  303.3 0.0 reduce-scatter.11.cloned.1.call-update
  303.3 2.8 multiply_reduce_fusion
  306.1 73.2 %psum.15 = f32[16,128]{1,0:T(8,128)S(1)} all-reduce(f32[16,128]{1,0:T(8,128)S(1)} %multiply_reduce_fusion), channel_id=1, replica_groups=mesh['rows'=8,'cols'=32] {'rows','cols'}, use_global_device_ids=true, to_apply=%region_9.0 | all-reduce | flops 2048 | bytes 16384 | tf_op jit(solution)/shard_map/psum | solution.py:41
  379.4 0.6 multiply_subtract_fusion.2
  380.0 25.9 %reduce-scatter.9.cloned.1.call-done = f32[16,128]{1,0:T(8,128)} async-done(((f32[512,128]{1,0:T(8,128)}), f32[16,128]{1,0:T(8,128)}) %reduce-scatter.9.cloned.1.call-update) | async-done | bytes 8208 | tf_op jit(solution)/shard_map/reduce_scatter | solution.py:37
  405.9 0.0 copy-done.6
  405.9 1.3 multiply_subtract_fusion.3
  407.2 40.1 %reduce-scatter.11.cloned.1.call-done = f32[64,128]{1,0:T(8,128)} async-done(((f32[512,128]{1,0:T(8,128)}), f32[64,128]{1,0:T(8,128)}) %reduce-scatter.11.cloned.1.call-update) | async-done | bytes 32784 | tf_op jit(solution)/shard_map/reduce_scatter | solution.py:38
  447.3 0.0 copy-done.3
  447.3 1.4 multiply_subtract_fusion
  (5 shorter events, 0.0 us)
Async XLA Ops:
  7.2 12.0 %copy-start.2 = (f32[64,128]{1,0:T(8,128)S(1)}, f32[64,128]{1,0:T(8,128)}, u32[]{:S(2)}) copy-start(f32[64,128]{1,0:T(8,128)} %param.6) | copy-start | bytes 98308
  7.2 40.7 %copy-start.4 = (f32[16,128]{1,0:T(8,128)S(1)}, f32[16,128]{1,0:T(8,128)}, u32[]{:S(2)}) copy-start(f32[16,128]{1,0:T(8,128)} %param.5) | copy-start | bytes 24580
  7.2 83.2 %copy-start.5 = (f32[16,128]{1,0:T(8,128)S(1)}, f32[16,128]{1,0:T(8,128)}, u32[]{:S(2)}) copy-start(f32[16,128]{1,0:T(8,128)} %param.7) | copy-start | bytes 24580
  7.2 205.1 %reduce-scatter.5.cloned.1.call-start = ((), (), s32[]{:S(2)}) async-start(), calls=%async_computation.4 | async-start | bytes 270336 | tf_op jit(solution)/shard_map/reduce_scatter | solution.py:37
  95.8 3.2 copy-start
  102.1 151.7 %reduce-scatter.7.cloned.1.call-start = ((), (), s32[]{:S(2)}) async-start(), calls=%async_computation.5 | async-start | bytes 294912 | tf_op jit(solution)/shard_map/reduce_scatter | solution.py:38
  110.5 295.3 %reduce-scatter.9.cloned.1.call-start = ((), (), s32[]{:S(2)}) async-start(), calls=%async_computation.6 | async-start | bytes 270336 | tf_op jit(solution)/shard_map/reduce_scatter | solution.py:37
  288.5 3.2 copy-start.1
  294.8 152.5 %reduce-scatter.11.cloned.1.call-start = ((), (), s32[]{:S(2)}) async-start(), calls=%async_computation.7 | async-start | bytes 294912 | tf_op jit(solution)/shard_map/reduce_scatter | solution.py:38
  303.3 102.6 %copy-start.6 = (f32[16,128]{1,0:T(8,128)S(1)}, f32[16,128]{1,0:T(8,128)}, u32[]{:S(2)}) copy-start(f32[16,128]{1,0:T(8,128)} %reduce-scatter.5.cloned.1.call-done) | copy-start | bytes 24580
  303.3 144.0 %copy-start.3 = (f32[64,128]{1,0:T(8,128)S(1)}, f32[64,128]{1,0:T(8,128)}, u32[]{:S(2)}) copy-start(f32[64,128]{1,0:T(8,128)} %reduce-scatter.7.cloned.1.call-done) | copy-start | bytes 98308
Sparse Core Ops, SparseCore 0:
  102.2 110.0 reduce-scatter.4
  214.8 38.9 reduce-scatter.6
  294.9 110.8 reduce-scatter.8
  408.4 38.8 reduce-scatter.10
where the time goes:
time: 456 us; the launch traced here: 455 us
  blocking collectives  288 us (63%)
  waiting for transfers between devices  90.7 us (20%)
  matrix products  33 us (7%)
  local copies, waits for them, and re-layouts  18.4 us (4%)
  between operations  13.9 us (3%)
  other arithmetic  11.1 us (2%)
    psum x2, blocking collectives, local(): summed_c = lax.psum(grad_c, ('rows', 'cols'))  150 us
    all_gather x2, blocking collectives, local(): lax.all_gather(local_a.astype(jnp.bfloat16), 'cols', axis=0, tiled=True)  80.5 us
    all_gather x2, blocking collectives, local(): lax.all_gather(local_b.astype(jnp.bfloat16), 'rows', axis=0, tiled=True)  57.1 us
    reduce_scatter x2, waiting for transfers between devices, local(): summed_a = lax.psum_scatter(grad_a, 'cols', scatter_dimension=0, tiled=True)  47.7 us
    reduce_scatter x2, waiting for transfers between devices, local(): summed_b = lax.psum_scatter(grad_b, 'rows', scatter_dimension=0, tiled=True)  42.9 us
    unnamed x15, local copies, waits for them, and re-layouts  18.4 us
    dot_general x2, matrix products, local(): lax.dot_general(residual, low_a, (((0,), (0,)), ((), ())), preferred_elem...  16.8 us
    dot_general x2, matrix products, local(): lax.dot_general(low_a, scaled, (((1,), (1,)), ((), ())), preferred_elemen...  10.1 us
  transfers between devices with their start and end apart: 4, of which 4 were waited for; matrix products, arithmetic and copies ran while one was open for 5% of the time, Pallas kernels for 0%

commit v1 on v0

--- a/solution.py
+++ b/solution.py
@@ -18,7 +18,12 @@
     rate_c = 0.3 / math.sqrt(total_i * total_j)
     local_a, local_b, shared_c = (start_a, start_b, start_c)
     for iteration in range(ITERS):
-        low_a = lax.all_gather(local_a.astype(jnp.bfloat16), "cols", axis=0, tiled=True)
+        low_a = jnp.concatenate(
+            lax.all_to_all(
+                jnp.stack([local_a.astype(jnp.bfloat16)] * lax.axis_size("cols")), "cols", 0, 0
+            ),
+            axis=0,
+        )
         low_b = lax.all_gather(local_b.astype(jnp.bfloat16), "rows", axis=0, tiled=True)
         low_b_wide = low_b.astype(jnp.float32)
         scaled = (low_b_wide[:, None, :] * shared_c[None, :, :]).astype(jnp.bfloat16)

time: 456 us -> 433 us (0.950)
  blocking collectives: 288 us -> 206 us
  waiting for transfers between devices: 90.7 us -> 120 us
  starting transfers between devices: 0.16 us -> 18.7 us
  matrix products: 33 us -> 43.2 us
    all_gather x2 -> x0, blocking collectives: 80.5 us -> none  [local(): lax.all_gather(local_a.astype(jnp.bfloat16), 'cols', axis=0, tiled=True)]
    reduce_scatter x2, waiting for transfers between devices: 42.9 us -> 72.9 us  [local(): summed_b = lax.psum_scatter(grad_b, 'rows', scatter_dimension=0, tiled=True)]
    all_to_all x0 -> x2, starting transfers between devices: none -> 18.4 us  [local(): lax.all_to_all(jnp.stack([local_a.astype(jnp.bfloat16)] * lax.axis_size('...]
    dot_general x2, matrix products: 16.8 us -> 27.1 us  [local(): lax.dot_general(residual, low_a, (((0,), (0,)), ((), ())), preferred_elem...]
    reduce_sum x2 -> x0, other arithmetic: 5.57 us -> none  [local(): grad_c = jnp.sum(mixed * low_b_wide[:, None, :], axis=0)]
  transfers between devices with their start and end apart: 4 -> 6, of which waited for: 4 -> 4; matrix products, arithmetic and copies ran while one was open for 5% -> 11% of each run, Pallas kernels for 0% -> 0%
where the time goes in v1:
time: 433 us; the launch traced here: 432 us
  blocking collectives  206 us (48%)
  waiting for transfers between devices  120 us (28%)
  matrix products  43.2 us (10%)
  local copies, waits for them, and re-layouts  22.5 us (5%)
  starting transfers between devices  18.7 us (4%)
  between operations  13.9 us (3%)
  other arithmetic  7.91 us (2%)
    psum x2, blocking collectives, local(): summed_c = lax.psum(grad_c, ('rows', 'cols'))  148 us
    reduce_scatter x2, waiting for transfers between devices, local(): summed_b = lax.psum_scatter(grad_b, 'rows', scatter_dimension=0, tiled=True)  72.9 us
    all_gather x2, blocking collectives, local(): lax.all_gather(local_b.astype(jnp.bfloat16), 'rows', axis=0, tiled=True)  57.3 us
    reduce_scatter x2, waiting for transfers between devices, local(): summed_a = lax.psum_scatter(grad_a, 'cols', scatter_dimension=0, tiled=True)  47.5 us
    dot_general x2, matrix products, local(): lax.dot_general(residual, low_a, (((0,), (0,)), ((), ())), preferred_elem...  27.1 us
    unnamed x15, local copies, waits for them, and re-layouts  18.4 us
    all_to_all x2, starting transfers between devices, local(): lax.all_to_all(jnp.stack([local_a.astype(jnp.bfloat16)] * lax.axis_size('...  18.4 us
    dot_general x2, matrix products, local(): lax.dot_general(low_a, scaled, (((1,), (1,)), ((), ())), preferred_elemen...  9.99 us
  transfers between devices with their start and end apart: 6, of which 4 were waited for; matrix products, arithmetic and copies ran while one was open for 11% of the time, Pallas kernels for 0%

profile of v1, /device:TPU:32, one launch (start us, length us, event | category | flops | bytes accessed | tf_op | source)
XLA Modules:
  0.0 432.4 jit_solution(14409933941166641745)
XLA Ops:
  7.2 0.7 convert_element_type.60
  7.9 0.7 stack.4
  8.5 11.2 %all-to-all-start = ((bf16[32,16,128]{2,1,0:T(8,128)(2,1)}), bf16[32,16,128]{2,1,0:T(8,128)(2,1)S(1)}, u32[]{:S(2)}, u32[]{:S(2)}) async-start(bf16[32,16,128]{2,1,0:T(8,128)(2,1)} %stack.4), calls=%async_computation | async-start | bytes 262144 | tf_op jit(solution)/shard_map/all_to_all | solution.py:22
  19.7 0.0 reduce-scatter.5.cloned.1.call-start
  19.8 0.8 convert_element_type.56
  20.6 28.6 %all_gather.6 = bf16[512,128]{1,0:T(8,128)(2,1)S(1)} all-gather(bf16[64,128]{1,0:T(8,128)(2,1)S(1)} %convert_element_type.56), channel_id=1, replica_groups=mesh['rows'=8,'cols'=32] {'rows'}, dimensions={0}, use_global_device_ids=true | all-gather | bytes 147456 | tf_op jit(solution)/shard_map/all_gather | solution.py:27
  49.2 1.2 multiply_convert_fusion.1
  50.4 1.4 copy.11
  51.7 12.0 %copy.12 = bf16[512,8192]{0,1:T(8,128)(2,1)} copy(bf16[512,8192]{1,0:T(8,128)(2,1)} %param.4) | data formatting | bytes 16777216 | tf_op args[0]
  63.7 0.0 all-to-all-done
  63.7 5.0 %fusion = bf16[512,8192]{0,1:T(8,128)(2,1)S(1)} fusion(bf16[512,8192]{0,1:T(8,128)(2,1)} %copy.12, bf16[8192,128]{1,0:T(8,128)(2,1)S(1)} %bitcast.27, bf16[512,128]{1,0:T(8,128)(2,1)S(1)} %bitcast.34), kind=kOutput, calls=%fused_computation.2 | convolution fusion | flops 1086324736 | bytes 19005440 | tf_op jit(solution)/shard_map/dot_general | solution.py:31
  68.7 0.0 copy-start
  68.7 3.2 copy-done
  71.9 0.0 copy-start.5
  71.9 3.1 fusion.8
  75.0 0.0 reduce-scatter.5.cloned.1.call-update
  75.0 0.2 reduce-scatter.7.cloned.1.call-start
  75.2 0.0 copy-done.5
  75.2 0.0 copy-start.4
  75.3 0.0 copy-start.2
  75.3 13.5 %multiply_reduce_fusion.3 = (f32[512,128]{1,0:T(8,128)}, f32[16,128]{1,0:T(8,128)S(1)}) fusion(f32[16,128]{1,0:T(8,128)S(1)} %copy-done.5, f32[512,128]{1,0:T(8,128)S(1)} %convert_element_type.57, bf16[512,128,1]{1,0,2:T(8,128)(2,1)S(1)} %bitcast.35, bf16[512,16,512]{2,1,0:T(8,128)(2,1)} %bitcast.26), kind=kOutput, calls=%fused_computation.12 | convolution fusion | flops 1077868544 | bytes 9060352 | tf_op jit(solution)/shard_map/dot_general | solution.py:36
  88.8 0.0 reduce-scatter.7.cloned.1.call-update
  88.8 75.3 %psum.14 = f32[16,128]{1,0:T(8,128)S(1)} all-reduce(f32[16,128]{1,0:T(8,128)S(1)} %get-tuple-element.6), channel_id=1, replica_groups=mesh['rows'=8,'cols'=32] {'rows','cols'}, use_global_device_ids=true, to_apply=%region_4.0 | all-reduce | flops 2048 | bytes 16384 | tf_op jit(solution)/shard_map/psum | solution.py:46
  164.2 24.0 %reduce-scatter.5.cloned.1.call-done = f32[16,128]{1,0:T(8,128)} async-done(((f32[512,128]{1,0:T(8,128)}), f32[16,128]{1,0:T(8,128)}) %reduce-scatter.5.cloned.1.call-update) | async-done | bytes 8208 | tf_op jit(solution)/shard_map/reduce_scatter | solution.py:42
  188.1 0.0 copy-done.4
  188.1 0.7 fusion.7
  188.8 0.7 stack.5
  189.5 7.2 %all-to-all-start.1 = ((bf16[32,16,128]{2,1,0:T(8,128)(2,1)}), bf16[32,16,128]{2,1,0:T(8,128)(2,1)S(1)}, u32[]{:S(2)}, u32[]{:S(2)}) async-start(bf16[32,16,128]{2,1,0:T(8,128)(2,1)} %stack.5), calls=%async_computation.2 | async-start | bytes 262144 | tf_op jit(solution)/shard_map/all_to_all | solution.py:22
  196.7 0.0 reduce-scatter.9.cloned.1.call-start
  196.8 32.8 %reduce-scatter.7.cloned.1.call-done = f32[64,128]{1,0:T(8,128)} async-done(((f32[512,128]{1,0:T(8,128)}), f32[64,128]{1,0:T(8,128)}) %reduce-scatter.7.cloned.1.call-update) | async-done | bytes 32784 | tf_op jit(solution)/shard_map/reduce_scatter | solution.py:43
  229.5 0.0 copy-done.2
  229.5 0.8 fusion.6
  230.3 28.7 %all_gather.7 = bf16[512,128]{1,0:T(8,128)(2,1)S(1)} all-gather(bf16[64,128]{1,0:T(8,128)(2,1)S(1)} %fusion.6), channel_id=1, replica_groups=mesh['rows'=8,'cols'=32] {'rows'}, dimensions={0}, use_global_device_ids=true | all-gather | bytes 147456 | tf_op jit(solution)/shard_map/all_gather | solution.py:27
  259.0 0.5 multiply_convert_fusion
  259.5 1.4 copy.14
  260.8 0.0 all-to-all-done.1
  260.8 5.0 %fusion.1 = bf16[512,8192]{0,1:T(8,128)(2,1)S(1)} fusion(bf16[512,8192]{0,1:T(8,128)(2,1)} %copy.12, bf16[512,128]{1,0:T(8,128)(2,1)S(1)} %bitcast.32, bf16[8192,128]{1,0:T(8,128)(2,1)S(1)} %bitcast.30), kind=kOutput, calls=%fused_computation.3 | convolution fusion | flops 1086324736 | bytes 19005440 | tf_op jit(solution)/shard_map/dot_general | solution.py:31
  265.8 0.0 copy-start.1
  265.8 3.2 copy-done.1
  269.1 3.1 fusion.9
  272.1 0.0 reduce-scatter.9.cloned.1.call-update
  272.1 0.0 reduce-scatter.11.cloned.1.call-start
  272.2 0.0 copy-start.6
  272.2 0.0 copy-start.3
  272.2 13.6 %multiply_reduce_fusion = (f32[16,128]{1,0:T(8,128)S(1)}, f32[512,128]{1,0:T(8,128)}) fusion(f32[512,128]{1,0:T(8,128)S(1)} %convert_element_type.65, f32[16,128]{1,0:T(8,128)S(1)} %multiply_subtract_fusion.4, bf16[512,128,1]{1,0,2:T(8,128)(2,1)S(1)} %bitcast.33, bf16[512,16,512]{2,1,0:T(8,128)(2,1)} %bitcast.29), kind=kOutput, calls=%fused_computation.8 | convolution fusion | flops 1077868544 | bytes 9060352 | tf_op jit(solution)/shard_map/dot_general | solution.py:36
  285.8 0.0 reduce-scatter.11.cloned.1.call-update
  285.8 73.1 %psum.15 = f32[16,128]{1,0:T(8,128)S(1)} all-reduce(f32[16,128]{1,0:T(8,128)S(1)} %get-tuple-element.3), channel_id=1, replica_groups=mesh['rows'=8,'cols'=32] {'rows','cols'}, use_global_device_ids=true, to_apply=%region_9.0 | all-reduce | flops 2048 | bytes 16384 | tf_op jit(solution)/shard_map/psum | solution.py:46
  358.9 0.6 multiply_subtract_fusion.2
  359.5 23.6 %reduce-scatter.9.cloned.1.call-done = f32[16,128]{1,0:T(8,128)} async-done(((f32[512,128]{1,0:T(8,128)}), f32[16,128]{1,0:T(8,128)}) %reduce-scatter.9.cloned.1.call-update) | async-done | bytes 8208 | tf_op jit(solution)/shard_map/reduce_scatter | solution.py:42
  383.1 0.0 copy-done.6
  383.1 1.3 multiply_subtract_fusion.3
  384.4 40.1 %reduce-scatter.11.cloned.1.call-done = f32[64,128]{1,0:T(8,128)} async-done(((f32[512,128]{1,0:T(8,128)}), f32[64,128]{1,0:T(8,128)}) %reduce-scatter.11.cloned.1.call-update) | async-done | bytes 32784 | tf_op jit(solution)/shard_map/reduce_scatter | solution.py:43
  424.5 0.0 copy-done.3
  424.5 1.4 multiply_subtract_fusion
  (3 shorter events, 0.0 us)
Async XLA Ops:
  8.5 55.2 %all-to-all-start = ((bf16[32,16,128]{2,1,0:T(8,128)(2,1)}), bf16[32,16,128]{2,1,0:T(8,128)(2,1)S(1)}, u32[]{:S(2)}, u32[]{:S(2)}) async-start(bf16[32,16,128]{2,1,0:T(8,128)(2,1)} %stack.4), calls=%async_computation | async-start | bytes 262144 | tf_op jit(solution)/shard_map/all_to_all | solution.py:22
  19.7 168.4 %reduce-scatter.5.cloned.1.call-start = ((), (), s32[]{:S(2)}) async-start(), calls=%async_computation.6 | async-start | bytes 270336 | tf_op jit(solution)/shard_map/reduce_scatter | solution.py:42
  68.7 3.2 copy-start
  71.9 3.3 copy-start.5
  75.0 154.5 %reduce-scatter.7.cloned.1.call-start = ((), (), s32[]{:S(2)}) async-start(), calls=%async_computation.7 | async-start | bytes 294912 | tf_op jit(solution)/shard_map/reduce_scatter | solution.py:43
  75.2 112.9 %copy-start.4 = (f32[16,128]{1,0:T(8,128)S(1)}, f32[16,128]{1,0:T(8,128)}, u32[]{:S(2)}) copy-start(f32[16,128]{1,0:T(8,128)} %param.5) | copy-start | bytes 24580
  75.3 154.3 %copy-start.2 = (f32[64,128]{1,0:T(8,128)S(1)}, f32[64,128]{1,0:T(8,128)}, u32[]{:S(2)}) copy-start(f32[64,128]{1,0:T(8,128)} %param.6) | copy-start | bytes 98308
  189.5 71.3 %all-to-all-start.1 = ((bf16[32,16,128]{2,1,0:T(8,128)(2,1)}), bf16[32,16,128]{2,1,0:T(8,128)(2,1)S(1)}, u32[]{:S(2)}, u32[]{:S(2)}) async-start(bf16[32,16,128]{2,1,0:T(8,128)(2,1)} %stack.5), calls=%async_computation.2 | async-start | bytes 262144 | tf_op jit(solution)/shard_map/all_to_all | solution.py:22
  196.7 186.4 %reduce-scatter.9.cloned.1.call-start = ((), (), s32[]{:S(2)}) async-start(), calls=%async_computation.8 | async-start | bytes 270336 | tf_op jit(solution)/shard_map/reduce_scatter | solution.py:42
  265.8 3.2 copy-start.1
  272.1 152.3 %reduce-scatter.11.cloned.1.call-start = ((), (), s32[]{:S(2)}) async-start(), calls=%async_computation.9 | async-start | bytes 294912 | tf_op jit(solution)/shard_map/reduce_scatter | solution.py:43
  272.2 110.9 %copy-start.6 = (f32[16,128]{1,0:T(8,128)S(1)}, f32[16,128]{1,0:T(8,128)}, u32[]{:S(2)}) copy-start(f32[16,128]{1,0:T(8,128)} %reduce-scatter.5.cloned.1.call-done) | copy-start | bytes 24580
  272.2 152.3 %copy-start.3 = (f32[64,128]{1,0:T(8,128)S(1)}, f32[64,128]{1,0:T(8,128)}, u32[]{:S(2)}) copy-start(f32[64,128]{1,0:T(8,128)} %reduce-scatter.7.cloned.1.call-done) | copy-start | bytes 98308
Sparse Core Ops, SparseCore 0:
  75.1 112.9 reduce-scatter.4
  190.6 38.8 reduce-scatter.6
  272.3 110.7 reduce-scatter.8
  385.6 38.8 reduce-scatter.10
